TPU v7x, 32 devices: a whole 2x2x4 slice. The times are simulated.
32 devices in a mesh: groups: 1, row: 8 (over z, y), col: 4 (over x, core).
Axes of the slice: x: 2, y: 2, z: 4, core: 2. Of those that a mesh axis runs over, the one named last changes fastest.
Arguments:
- activations: bfloat16 [1024, 16384], P('groups', ('row', 'col')), may hold values from -2.5 to 2.5
- token_ids: int32 [1024], P('groups'), may hold values from 0 to 128255
- initial: float32 [16384, 256], P(('groups', 'row', 'col')), may hold values from -6 to 6
- block_mask: int32 [128, 2], P('groups'), may hold values 0 or 1
Outputs:
- gram: float32 [8, 4, 512, 16384], P('groups', 'col', None, 'row')
- repaired: float32 [16384, 256], P(('groups', 'row', 'col'))
All inputs are finite; a program needn't handle non-finite values.
Results may differ from a plain program's by a relative error of at most 0.0003.
Values may be sent and summed in bfloat16 or wider, within the bound.
No kernel may reach another device: no remote copies, remote signals or barrier semaphores. Data moves between devices by JAX's collectives and lax.ppermute only.
A program may use at most 128 MiB of HBM per device.

v0:
```python
import math

import jax
import jax.numpy as jnp
from jax import lax
from jax.sharding import PartitionSpec as P

D = 16384
ROWS = 1024
BLOCK = 128
ITERS = 2


def shards(activations, token_ids, initial, block_mask):
    matches = (token_ids[:, None] == token_ids[None, :]).astype(jnp.float32)
    weights = 1.0 / jnp.sum(matches, axis=1)
    weighted = (activations.astype(jnp.float32) * weights[:, None]).astype(jnp.bfloat16)
    column_panel = lax.all_gather(activations, "col", axis=1, tiled=True)
    gram_tile = lax.dot_general(
        lax.all_gather(weighted, "row", axis=1, tiled=True),
        column_panel,
        (((0,), (0,)), ((), ())),
        preferred_element_type=jnp.float32,
    ) * (1.0 / ROWS)
    shard_rows = initial.shape[0]
    col_count = lax.axis_size("col")
    first_feature = (lax.axis_index("row") * col_count + lax.axis_index("col")) * shard_rows
    block_index = (first_feature + jnp.arange(shard_rows, dtype=jnp.int32)) // BLOCK
    selector = (
        block_index[:, None] == jnp.arange(block_mask.shape[0], dtype=jnp.int32)[None, :]
    ).astype(jnp.float32)
    mask_rows = jnp.dot(selector, block_mask.astype(jnp.float32), precision=lax.Precision.HIGHEST)
    mask_full = jnp.repeat(mask_rows, BLOCK, axis=1)
    step_size = ROWS / (D + 2.0 * math.sqrt(D * ROWS) + ROWS)
    current = mask_full * initial
    for iteration in range(ITERS):
        change_now = current - initial
        projected = jnp.dot(
            activations.astype(jnp.float32), change_now, precision=lax.Precision.HIGHEST
        )
        totals = lax.psum(projected, ("row", "col"))
        pulled = lax.dot_general(
            weighted.astype(jnp.float32),
            totals,
            (((0,), (0,)), ((), ())),
            precision=lax.Precision.HIGHEST,
        ) * (1.0 / ROWS)
        current = mask_full * (current - step_size * pulled)
    gram_out = gram_tile.reshape(lax.axis_size("row"), 1, shard_rows, gram_tile.shape[1])
    return (gram_out, current)


def solution(mesh):
    in_specs = (
        P("groups", ("row", "col")),
        P("groups"),
        P(("groups", "row", "col"), None),
        P("groups", None),
    )
    out_specs = (P("groups", "col", None, "row"), P(("groups", "row", "col"), None))
    return jax.shard_map(shards, mesh=mesh, in_specs=in_specs, out_specs=out_specs, check_vma=False)
```

profile of v0, /device:TPU:0, one launch (start us, length us, event | category | flops | bytes accessed | tf_op | source)
XLA Modules:
  0.0 426.7 jit_solution(2539099986985370560)
XLA Ops:
  8.0 0.0 copy-start
  8.0 0.0 copy-start.2
  8.0 0.0 all-reduce.3.cloned.1.call-start
  8.1 1.1 fusion.8
  9.2 0.6 broadcast_in_dim.2
  9.8 4.3 %convolution_bitcast_fusion.1 = f32[1024,256]{0,1:T(8,128)} fusion(bf16[1024,512]{1,0:T(8,128)(2,1)} %param.4, f32[512,256]{1,0:T(8,128)} %param.6, f32[64,8,2,128]{3,2,1,0:T(2,128)S(1)} %bitcast.25), kind=kOutput, calls=%fused_computation.4 | convolution fusion | flops 1610874880 | bytes 3145728 | tf_op jit(solution)/shard_map/dot_general | solution.py:38
  14.1 0.0 all-reduce.3.cloned.1.call-update
  14.1 0.0 all-reduce.5.cloned.1.call-start
  14.1 0.0 copy-done.2
  14.1 0.5 convert_reduce_fusion
  14.7 0.0 copy-done
  14.7 0.3 multiply_convert_fusion
  15.0 0.0 copy-start.1
  15.0 132.6 %all-reduce.3.cloned.1.call-done = f32[1024,256]{0,1:T(8,128)} async-done(((f32[1024,256]{0,1:T(8,128)}), f32[1024,256]{0,1:T(8,128)}) %all-reduce.3.cloned.1.call-update) | async-done | bytes 1048592 | tf_op jit(solution)/shard_map/psum | solution.py:41
  147.6 2.6 fusion.1
  150.3 3.9 convolution_bitcast_fusion
  154.1 0.0 all-reduce.5.cloned.1.call-update
  154.2 0.0 all-gather.5.cloned.1.call-start
  154.2 0.5 all-gather.5.cloned.1.call-update
  154.7 0.0 copy-done.1
  154.7 0.2 all-gather.3.cloned.1.call-start
  155.0 0.4 all-gather.3.cloned.1.call-update
  155.3 234.5 %all-reduce.5.cloned.1.call-done = f32[1024,256]{0,1:T(8,128)} async-done(((f32[1024,256]{0,1:T(8,128)}), f32[1024,256]{0,1:T(8,128)}) %all-reduce.5.cloned.1.call-update) | async-done | bytes 1048592 | tf_op jit(solution)/shard_map/psum | solution.py:41
  389.9 3.6 fusion.3
  393.5 0.0 all-gather.5.cloned.1.call-done
  393.5 0.0 all-gather.3.cloned.1.call-done
  393.5 25.8 %convolution_multiply_fusion = f32[4096,2048]{1,0:T(8,128)} fusion(bf16[1024,4096]{1,0:T(8,128)(2,1)} %all-gather.3.cloned.1.call-done, bf16[1024,2048]{1,0:T(8,128)(2,1)} %all-gather.5.cloned.1.call-done), kind=kOutput, calls=%fused_computation | convolution fusion | flops 17188257792 | bytes 46137344 | tf_op jit(solution)/shard_map/dot_general | solution.py:19
  (2 shorter events, 0.0 us)
Async XLA Ops:
  8.0 6.7 %copy-start = (bf16[1024,512]{1,0:T(8,128)(2,1)S(1)}, bf16[1024,512]{1,0:T(8,128)(2,1)}, u32[]{:S(2)}) copy-start(bf16[1024,512]{1,0:T(8,128)(2,1)} %param.4) | copy-start | bytes 3145732
  8.0 6.1 %copy-start.2 = (s32[1024]{0:T(1024)S(1)}, s32[1024]{0:T(1024)}, u32[]{:S(2)}) copy-start(s32[1024]{0:T(1024)} %param.5) | copy-start | bytes 12292
  8.0 139.6 %all-reduce.3.cloned.1.call-start = ((), (), s32[]{:S(2)}) async-start(), calls=%async_computation.2 | async-start | bytes 2097152 | tf_op jit(solution)/shard_map/psum | solution.py:41
  14.1 375.8 %all-reduce.5.cloned.1.call-start = ((), (), s32[]{:S(2)}) async-start(), calls=%async_computation.3 | async-start | bytes 2097152 | tf_op jit(solution)/shard_map/psum | solution.py:41
  15.0 139.7 %copy-start.1 = (bf16[1024,512]{1,0:T(8,128)(2,1)}, bf16[1024,512]{1,0:T(8,128)(2,1)S(1)}, u32[]{:S(2)}) copy-start(bf16[1024,512]{1,0:T(8,128)(2,1)S(1)} %multiply_convert_fusion) | copy-start | bytes 3145732
  154.2 239.3 %all-gather.5.cloned.1.call-start = ((), (), s32[]{:S(2)}) async-start(), calls=%async_computation.1 | async-start | bytes 5242880 | tf_op jit(solution)/shard_map/all_gather | solution.py:18
  154.7 238.7 %all-gather.3.cloned.1.call-start = ((), (), s32[]{:S(2)}) async-start(), calls=%async_computation | async-start | bytes 9437184 | tf_op jit(solution)/shard_map/all_gather | solution.py:20
Sparse Core Ops, SparseCore 0:
  14.2 133.3 all-reduce.2
  154.3 235.5 all-reduce.4
Sparse Core Ops, SparseCore 1:
  156.2 33.8 all-gather.4
  192.5 125.3 all-gather.2
where the time goes:
time: 427 us
  waiting for transfers between devices  368 us (86%)
  matrix products  41.3 us (10%)
  between operations  15.6 us (4%)
    psum x2, waiting for transfers between devices, shards(): totals = lax.psum(projected, ('row', 'col'))  367 us
    dot_general x1, matrix products, shards(): lax.dot_general(lax.all_gather(weighted, 'row', axis=1, tiled=True), colu...  25.8 us
  transfers between devices with their start and end apart: 4, of which 2 were waited for; matrix products, arithmetic and copies ran while one was open for 1% of the time, Pallas kernels for 0%

commit v1 on v0

v1 whole, which is shorter than its diff:
```python
import functools
import math

import jax
import jax.numpy as jnp
from jax import lax
from jax.experimental import pallas as pl
from jax.experimental.pallas import tpu as pltpu
from jax.sharding import PartitionSpec as P


BLOCK = 128
SLOTS = [0, 2, 3, 5, 4, 6, 10, 7, 8, 10, 11]


SMEM = pl.BlockSpec(memory_space=pltpu.SMEM)
VMEM = pl.BlockSpec(memory_space=pltpu.VMEM)
ANY = pl.BlockSpec(memory_space=pl.ANY)


def split3(value):
    high = value.astype(jnp.bfloat16)
    rest = value - high.astype(jnp.float32)
    middle = rest.astype(jnp.bfloat16)
    low = (rest - middle.astype(jnp.float32)).astype(jnp.bfloat16)
    return jnp.concatenate([high, middle, low], axis=0)


def sum3(value):
    third = value.shape[0] // 3
    return value[:third] + (value[third : 2 * third] + value[2 * third :])


def nt_dot(left, right):
    return lax.dot_general(left, right, (((1,), (1,)), ((), ())), preferred_element_type=jnp.float32)


def dot(left, right):
    return jnp.dot(left, right, preferred_element_type=jnp.float32)


def mib(count):
    return pltpu.CompilerParams(vmem_limit_bytes=count << 20)


def keep_give(value, mine, keep_ref, give_ref):
    half = value.shape[0] // 2
    low, high = value[:half], value[half:]
    first = mine == 0
    keep_ref[...] = jnp.where(first, low, high)
    give_ref[...] = jnp.where(first, high, low)


def lanes(column, width):
    if width <= column.shape[1]:
        return column[:, :width]
    return jnp.concatenate([column] * (width // column.shape[1]), axis=1)


def start_kernel(first_ref, mine_ref, mask_ref, ids_ref, act_in, initial_in, *refs):
    keep_ref, give_ref, act_ref, column_ref = refs[:4]
    piece_refs, (initial_ref, sems) = refs[4:-2], refs[-2:]
    act_copy = pltpu.make_async_copy(act_in, act_ref, sems.at[0])
    initial_copy = pltpu.make_async_copy(initial_in, initial_ref, sems.at[1])
    act_copy.start()
    initial_copy.start()
    rows = ids_ref.shape[1]
    ids = ids_ref[...].astype(jnp.float32)
    ids_column = jnp.broadcast_to(ids, (BLOCK, rows)).T
    counts = []
    for low in range(0, rows, BLOCK):
        same = jnp.where(ids_column == ids[:, low : low + BLOCK], 1.0, 0.0)
        counts.append(jnp.sum(same, axis=0, keepdims=True))
    weights = 1.0 / jnp.concatenate(counts, axis=1)
    column_ref[...] = jnp.broadcast_to(weights, (BLOCK, rows)).T
    initial_copy.wait()
    features, columns = initial_ref.shape
    step = min(BLOCK, features)
    stripes = []
    for low in range(0, features, step):
        blocks = []
        for o in range(columns // BLOCK):
            kept = mask_ref[o, first_ref[0] + low // step].astype(jnp.float32) - 1.0
            blocks.append(initial_ref[low : low + step, o * BLOCK : (o + 1) * BLOCK] * kept)
        stripes.append(jnp.concatenate(blocks, axis=1))
    change = split3(jnp.concatenate(stripes, axis=0).T)
    act_copy.wait()
    keep_give(sum3(nt_dot(change, act_ref[...])), mine_ref[0], keep_ref, give_ref)
    weighted = (act_ref[...].astype(jnp.float32).T * weights).astype(jnp.bfloat16)
    low = 0
    for piece_ref in piece_refs:
        piece_ref[...] = weighted[low : low + piece_ref.shape[0]]
        low += piece_ref.shape[0]


def start(first_block, mine, mask_t, token_ids, act, initial, heights):
    rows = act.shape[0]
    half = jax.ShapeDtypeStruct((initial.shape[1] // 2, rows), jnp.float32)
    shapes = [half, half, jax.ShapeDtypeStruct(act.shape, act.dtype)]
    shapes += [jax.ShapeDtypeStruct((rows, BLOCK), jnp.float32)]
    shapes += [jax.ShapeDtypeStruct((h, rows), jnp.bfloat16) for h in heights]
    return pl.pallas_call(
        start_kernel,
        out_shape=tuple(shapes),
        in_specs=[SMEM, SMEM, SMEM, VMEM, ANY, ANY],
        out_specs=(VMEM,) * len(shapes),
        scratch_shapes=[pltpu.VMEM(initial.shape, jnp.float32), pltpu.SemaphoreType.DMA((2,))],
        compiler_params=mib(24),
        name="start",
    )(first_block.reshape(1), mine.reshape(1), mask_t, token_ids[None, :], act, initial)


def fold_kernel(where_ref, held_ref, got_ref, keep_ref, give_ref):
    keep_give(held_ref[...] + got_ref[...], where_ref[0], keep_ref, give_ref)


def fold(held, got, mine):
    half = jax.ShapeDtypeStruct((held.shape[0] // 2, held.shape[1]), jnp.float32)
    return pl.pallas_call(
        fold_kernel,
        out_shape=(half, half),
        in_specs=[SMEM, VMEM, VMEM],
        out_specs=(VMEM, VMEM),
        compiler_params=mib(4),
        name="fold",
    )(mine.reshape(1), held, got)


def step_kernel(spots, given, where_ref, mask_ref, column_ref, *refs):
    total_refs, refs = refs[:given], refs[given:]
    count = len(spots)
    act_ins, out_refs, (act_refs, sems) = refs[:count], refs[count:-2], refs[-2:]
    copies = [pltpu.make_async_copy(act_ins[j], act_refs.at[j], sems.at[j]) for j in range(count)]
    for copy in copies:
        copy.start()
    features = act_refs.shape[2]
    step = min(BLOCK, features)
    pieces = split3(jnp.concatenate([ref[...] for ref in total_refs], axis=0))
    weights = lanes(column_ref[...], features)
    moved = None
    for j in range(count):
        copies[j].wait()
        act = act_refs[j]
        pulled = sum3(dot(pieces, (act.astype(jnp.float32) * weights).astype(jnp.bfloat16)))
        masked = []
        for low in range(0, features, step):
            kept = mask_ref[where_ref[spots[0] - 1], where_ref[spots[j]] + low // step].astype(jnp.float32)
            masked.append(pulled[:, low : low + step] * kept)
        part = sum3(nt_dot(split3(jnp.concatenate(masked, axis=1)), act))
        moved = part if moved is None else moved + part
    share = out_refs[0].shape[0]
    for i, out_ref in enumerate(out_refs):
        out_ref[...] = moved[i * share : (i + 1) * share]


def masked_step(where, spots, mask_t, column, totals, acts, scatter):
    columns, rows = sum(t.shape[0] for t in totals), totals[0].shape[1]
    outputs = 2 if scatter else 1
    shape = jax.ShapeDtypeStruct((columns // outputs, rows), jnp.float32)
    return pl.pallas_call(
        functools.partial(step_kernel, spots, len(totals)),
        out_shape=(shape,) * outputs,
        in_specs=[SMEM, SMEM, VMEM] + [VMEM] * len(totals) + [ANY] * len(acts),
        out_specs=(VMEM,) * outputs,
        scratch_shapes=[
            pltpu.VMEM((len(acts),) + acts[0].shape, acts[0].dtype),
            pltpu.SemaphoreType.DMA((len(acts),)),
        ],
        compiler_params=mib(24),
        name="masked_step",
    )(where, mask_t, column, *totals, *acts)


def finish_kernel(scale, first, spots, given, where_ref, mask_ref, initial_ref, *refs):
    sums_refs, weighted_refs, (out_ref, pieces_ref) = refs[:given], refs[given:-2], refs[-2:]
    columns = pieces_ref.shape[1]
    features = initial_ref.shape[0]
    piece = columns // len(spots)
    number = 0
    for sums_ref in sums_refs:
        for low in range(0, sums_ref.shape[0], piece):
            spot = pl.ds(pl.multiple_of(where_ref[spots[number]] * piece, piece), piece)
            value = sums_ref[low : low + piece, :]
            high = value.astype(jnp.bfloat16).astype(jnp.float32)
            rest = value - high
            middle = rest.astype(jnp.bfloat16).astype(jnp.float32)
            pieces_ref[0, spot, :] = high
            pieces_ref[1, spot, :] = middle
            pieces_ref[2, spot, :] = rest - middle
            number += 1
    pieces = pieces_ref[...].reshape(3 * columns, -1).astype(jnp.bfloat16)
    weighted = jnp.concatenate([ref[...] for ref in weighted_refs], axis=0)
    moved = sum3(nt_dot(pieces, weighted)).T * scale
    step = min(BLOCK, features)
    for low in range(0, features, step):
        for o in range(columns // BLOCK):
            kept = mask_ref[o, where_ref[first] + low // step].astype(jnp.float32)
            at = (slice(low, low + step), slice(o * BLOCK, (o + 1) * BLOCK))
            out_ref[at] = kept * (initial_ref[at] - moved[at])


def finish(where, first, spots, mask_t, initial, sums, weighted, scale):
    return pl.pallas_call(
        functools.partial(finish_kernel, scale, first, spots, len(sums)),
        out_shape=jax.ShapeDtypeStruct(initial.shape, jnp.float32),
        in_specs=[SMEM, SMEM] + [VMEM] * (1 + len(sums) + len(weighted)),
        out_specs=VMEM,
        scratch_shapes=[pltpu.VMEM((3, initial.shape[1], sums[0].shape[1]), jnp.float32)],
        compiler_params=mib(16),
        name="finish",
    )(where, mask_t, initial, *sums, *weighted)


def gram_kernel(scale, groups, panels, block, col, where_ref, *refs):
    parts = sum(len(group) for group in groups)
    weighted, acts = refs[:parts], refs[parts : parts + panels]
    out_ref, held, sems = refs[-3:]
    width = acts[0].shape[1]
    copies = []
    low = 0
    for group in groups:
        left = jnp.concatenate([weighted[i][...] for i in group], axis=0)
        height = left.shape[0]
        for j in range(panels):
            spot = 0 if panels == 1 else pl.multiple_of(jnp.bitwise_xor(where_ref[col], j) * width, width)
            held[j, low : low + height, :] = dot(left, acts[j][...]) * scale
            copy = pltpu.make_async_copy(
                held.at[j, pl.ds(low, height), :],
                out_ref.at[where_ref[block], 0, pl.ds(low, height), pl.ds(spot, width)],
                sems.at[len(copies)],
            )
            copy.start()
            copies.append(copy)
        low += height
    for copy in copies:
        copy.wait()


def gram_block(buffer, where, block, col, pieces, acts, blocks):
    rows = pieces[0].shape[1]
    features = sum(p.shape[0] for p in pieces)
    panels, width = len(acts), acts[0].shape[1]
    groups, size = [[]], 0
    for i, piece in enumerate(pieces):
        if size + piece.shape[0] > 256:
            groups.append([])
            size = 0
        groups[-1].append(i)
        size += piece.shape[0]
    operands = [where, *pieces, *acts]
    in_specs = [SMEM] + [VMEM] * (len(operands) - 1)
    aliases = {}
    if buffer is not None:
        in_specs.append(ANY)
        aliases = {len(operands): 0}
        operands.append(buffer)
    return pl.pallas_call(
        functools.partial(gram_kernel, 1.0 / rows, groups, panels, block, col),
        in_specs=in_specs,
        out_specs=ANY,
        out_shape=jax.ShapeDtypeStruct((blocks, 1, features, panels * width), jnp.float32),
        scratch_shapes=[
            pltpu.VMEM((panels, features, width), jnp.float32),
            pltpu.SemaphoreType.DMA((panels * len(groups),)),
        ],
        input_output_aliases=aliases,
        compiler_params=mib(12),
        cost_estimate=pl.CostEstimate(
            flops=2 * features * rows * panels * width,
            bytes_accessed=4 * features * panels * width,
            transcendentals=0,
        ),
    )(*operands)


def after(value, *others):
    if not others:
        return value
    return lax.optimization_barrier((value, *others))[0]


def bits(size):
    return [1 << i for i in range(size.bit_length() - 1)]


def plan(row_count, col_count, features, scatter):
    heights = [features // 2, features // 4, features // 4] if features % 64 == 0 else [features]
    half = row_count // 2
    units = []
    for step in range(1, half):
        for i in range(len(heights)):
            units.append([(i, step, 1), (i, step, -1)])
    if len(heights) == 3:
        units.append([(0, half, 1), (1, half, -1)])
        units.append([(2, half, -1)])
    else:
        units.append([(0, half, 1)])
    cols, rows = bits(col_count), bits(row_count)
    sums = [("row", bit) for bit in rows] + ([("row", 1)] if scatter else [])
    hops = [("col", bit) for bit in cols] + sums + sums
    hops += [("col", bit) for bit in reversed(cols)]
    if (row_count, col_count) == (8, 4):
        slots = SLOTS
    else:
        slots = [k * (len(hops) - 1) // len(units) for k in range(len(units))]
    return heights, units, hops, slots


def shards(activations, token_ids, initial, block_mask):
    rows, features = activations.shape
    row_count, col_count = lax.axis_size("row"), lax.axis_size("col")
    columns = initial.shape[1]
    row, col = lax.axis_index("row"), lax.axis_index("col")
    depth = row_count * col_count * features
    step_size = rows / (depth + 2.0 * math.sqrt(depth * rows) + rows)
    scatter = (columns // col_count) % 16 == 0
    heights, units, hops, slots = plan(row_count, col_count, features, scatter)
    cols = bits(col_count)
    half = row_count // 2
    mask_t = block_mask.T

    order = list(range(0, row_count, 2)) + list(range(row_count - 1, 0, -2))
    forward = [(order[i], order[(i + 1) % row_count]) for i in range(row_count)]
    backward = [(b, a) for a, b in forward]
    tail = ([("row", 1)] if scatter else []) + [("col", bit) for bit in reversed(cols)]
    table = []
    for r in range(row_count):
        for c in range(col_count):
            first_column, width = 0, columns
            for bit in cols:
                width //= 2
                first_column += (c // bit) % 2 * width
            entries = [(r * col_count + c) * features // BLOCK, c, first_column // BLOCK]
            entries += [(r * col_count + (c ^ j)) * features // BLOCK for j in range(col_count)]
            entries += [order[(order.index(r) - s) % row_count] for s in range(row_count)]
            for i in range(1 << len(tail)):
                spot = 0
                for t, (axis, bit) in enumerate(tail):
                    spot += ((r if axis == "row" else c) // bit % 2 ^ (i >> t) & 1) << t
                entries.append(spot)
            table.append(entries)
    where = jnp.array(table, jnp.int32)[row * col_count + col]
    step_spots = [3 + j for j in range(col_count)]
    source_spot = 3 + col_count
    piece_spots = [source_spot + row_count + i for i in range(1 << len(tail))]

    def mine(axis, bit):
        return jnp.bitwise_and((row if axis == "row" else col) // bit, 1).astype(jnp.int32)

    first_block = ((row * col_count + col) * features // BLOCK).astype(jnp.int32)
    keep, give, own, column, *pieces = start(
        first_block, mine("col", cols[0]), mask_t, token_ids, activations, initial, heights
    )

    arrived = {(0, i): piece for i, piece in enumerate(pieces)}

    def send_unit(k, *gate):
        for i, step, way in units[k]:
            source = arrived[((step - 1) * way % row_count, i)]
            got = lax.ppermute(after(source, *gate), "row", forward if way > 0 else backward)
            arrived[(step * way % row_count, i)] = got

    def units_at(number, *gate):
        for k, slot in enumerate(slots):
            if slot == number:
                send_unit(k, *gate)

    acts = [own]

    def gather_col(bit, *gate):
        for value in list(acts):
            acts.append(lax.ppermute(after(value, *gate), "col", [(c, c ^ bit) for c in range(col_count)]))

    def hop(number, value):
        axis, bit = hops[number]
        size = lax.axis_size(axis)
        return lax.ppermute(value, axis, [(i, i ^ bit) for i in range(size)])

    units_at(-1)
    number = 0
    for position, bit in enumerate(cols):
        gate = give
        got = hop(number, give)
        units_at(number, gate)
        if position == len(cols) - 1:
            gather_col(bit, gate)
        number += 1
        if position + 1 < len(cols) or scatter:
            keep, give = fold(keep, got, mine(*hops[number]))
        else:
            keep = keep + got
    for bit in reversed(cols[:-1]):
        gather_col(bit, keep)
    codes = [0]
    for bit in reversed(cols):
        codes += [code ^ bit for code in codes]
    acts = [acts[codes.index(j)] for j in range(col_count)]

    def row_sum(number, keep, give):
        rest = bits(row_count)
        if scatter:
            gate = give
            got = hop(number, give)
            units_at(number, gate)
            keep = keep + got
            number += 1
            rest = rest[1:]
        for _ in rest:
            gate = keep
            got = hop(number, keep)
            units_at(number, gate)
            keep = keep + got
            number += 1
        return number, keep

    number, total = row_sum(number, keep, give)
    totals = [total]
    if scatter:
        totals.append(hop(number, total))
        units_at(number, total)
        number += 1
    moved = masked_step(where, step_spots, mask_t, column, totals, acts, scatter)
    number, change = row_sum(number, moved[0], moved[-1])
    sums = [total + (total - (step_size / rows) * change)]
    for _ in tail:
        value = sums[0] if len(sums) == 1 else jnp.concatenate(sums, axis=0)
        other = hop(number, value)
        units_at(number, value)
        sums = [value, other]
        number += 1
    repaired = finish(where, 0, piece_spots, mask_t, initial, sums, pieces, step_size / rows)

    panels = acts
    if features % BLOCK:
        panels = []
        for place in range(col_count):
            chosen = acts[0]
            for j in range(1, col_count):
                chosen = jnp.where(jnp.bitwise_xor(col, j) == place, acts[j], chosen)
            panels.append(chosen)
        panels = [jnp.concatenate(panels, axis=1)]
    arrival = [0]
    for step in range(1, half + 1):
        arrival += [step] if step == half else [step, row_count - step]
    gram = None
    for slot in arrival:
        blocks = [arrived[(slot, i)] for i in range(len(heights))]
        gram = gram_block(gram, where, source_spot + slot, 1, blocks, panels, row_count)
    return gram, repaired


def solution(mesh):
    in_specs = (
        P("groups", ("row", "col")),
        P("groups"),
        P(("groups", "row", "col"), None),
        P("groups", None),
    )
    out_specs = (P("groups", "col", None, "row"), P(("groups", "row", "col"), None))
    return jax.shard_map(shards, mesh=mesh, in_specs=in_specs, out_specs=out_specs, check_vma=False)
```

time: 427 us -> 176 us (0.41)
  waiting for transfers between devices: 368 us -> 77.5 us
  Pallas kernels: 0 us -> 45.5 us
  matrix products: 41.3 us -> 0 us
  starting transfers between devices: 0.35 us -> 37 us
  between operations: 15.6 us -> 1.18 us
  local copies, waits for them, and re-layouts: 0.62 us -> 14 us
    psum x2 -> x0, waiting for transfers between devices: 367 us -> none  [shards(): totals = lax.psum(projected, ('row', 'col'))]
    ppermute x0 -> x36, waiting for transfers between devices: none -> 77.5 us  [the longest x12 63.5 us: hop(): return lax.ppermute(value, axis, [(i, i ^ bit) for i in range(size)])]
    pallas_call x0 -> x13, Pallas kernels: none -> 45.5 us  [the longest x8 36 us: gram_block(): pl.pallas_call(functools.partial(gram_kernel, 1.0 / rows, groups, panels,...]
    dot_general x6 -> x0, matrix products: 41.3 us -> none  [the longest x1 25.8 us: shards(): lax.dot_general(lax.all_gather(weighted, 'row', axis=1, tiled=True), colu...]
    ppermute x0 -> x36, starting transfers between devices: none -> 37 us  [the longest x21 19.2 us: send_unit(): lax.ppermute(after(source, *gate), 'row', forward if way > 0 else backward)]
    unnamed x6 -> x36, local copies, waits for them, and re-layouts: 0.02 us -> 13.3 us
  transfers between devices with their start and end apart: 4 -> 36, of which waited for: 2 -> 14; matrix products, arithmetic and copies ran while one was open for 1% -> 0% of each run, Pallas kernels for 0% -> 22%
where the time goes in v1:
time: 176 us; the launch traced here: 175 us
  waiting for transfers between devices  77.5 us (44%)
  Pallas kernels  45.5 us (26%)
  starting transfers between devices  37 us (21%)
  local copies, waits for them, and re-layouts  14 us (8%)
    ppermute x12, waiting for transfers between devices, hop(): return lax.ppermute(value, axis, [(i, i ^ bit) for i in range(size)])  63.5 us
    pallas_call x8, Pallas kernels, gram_block(): pl.pallas_call(functools.partial(gram_kernel, 1.0 / rows, groups, panels,...  36 us
    ppermute x21, starting transfers between devices, send_unit(): lax.ppermute(after(source, *gate), 'row', forward if way > 0 else backward)  19.2 us
    ppermute x12, starting transfers between devices, hop(): return lax.ppermute(value, axis, [(i, i ^ bit) for i in range(size)])  14.4 us
    ppermute x21, waiting for transfers between devices, send_unit(): lax.ppermute(after(source, *gate), 'row', forward if way > 0 else backward)  14 us
    unnamed x36, local copies, waits for them, and re-layouts  13.3 us
    pallas_call x1, Pallas kernels, masked_step(): pl.pallas_call(functools.partial(step_kernel, spots, len(totals)), out_sh...  4.16 us
  transfers between devices with their start and end apart: 36, of which 14 were waited for; matrix products, arithmetic and copies ran while one was open for 0% of the time, Pallas kernels for 22%

profile of v1, /device:TPU:0, one launch (start us, length us, event | category | flops | bytes accessed | tf_op | source)
XLA Modules:
  0.0 175.3 jit_solution(9100246464560483983)
XLA Ops:
  4.3 2.5 %start.1 = (f32[128,1024]{1,0:T(8,128)S(1)}, f32[128,1024]{1,0:T(8,128)S(1)}, bf16[1024,512]{1,0:T(8,128)(2,1)S(1)}, f32[1024,128]{1,0:T(8,128)S(1)}, bf16[256,1...) custom-call(s32[1]{0:T(128)} %bitcast.1.first_ref, s32[1]{0:T(128)} %bitcast.2.mine_ref, ...), custom_call_target="tpu_custom_call" | custom-call | tf_op jit(solution)/shard_map/start/pallas_call | solution.py:102
  14.9 2.9 %collective-permute-start.9 = (bf16[1024,512]{1,0:T(8,128)(2,1)S(1)}, bf16[1024,512]{1,0:T(8,128)(2,1)S(1)}, u32[]{:S(2)}, u32[]{:S(2)}) collective-permute-start(bf16[1024,512]{1,0:T(8,128)(2,1)S(1)} %get-tuple-element.48.refs_2_.refs_3_), channel_id=1, source_target_pairs={{0,2},{1,3},{2,0},{3,1},{4,6},{5,7},{6,4},{7,5},{8,10},{9,11},{10,... | collective-permute-start | bytes 3145736 | tf_op jit(solution)/shard_map/ppermute | solution.py:372
  17.9 29.0 %collective-permute-done.2.got_ref = f32[64,1024]{1,0:T(8,128)S(1)} collective-permute-done((f32[64,1024]{1,0:T(8,128)S(1)}, f32[64,1024]{1,0:T(8,128)S(1)}, u32[]{:S(2)}, u32[]{:S(2)}) %collective-permute-start.2) | collective-permute-done | bytes 262176 | tf_op jit(solution)/shard_map/ppermute | solution.py:377
  49.3 3.7 %collective-permute-done.3 = f32[32,1024]{1,0:T(8,128)S(1)} collective-permute-done((f32[32,1024]{1,0:T(8,128)S(1)}, f32[32,1024]{1,0:T(8,128)S(1)}, u32[]{:S(2)}, u32[]{:S(2)}) %collective-permute-start.3) | collective-permute-done | bytes 131104 | tf_op jit(solution)/shard_map/ppermute | solution.py:377
  54.9 3.2 %collective-permute-done.4 = f32[32,1024]{1,0:T(8,128)S(1)} collective-permute-done((f32[32,1024]{1,0:T(8,128)S(1)}, f32[32,1024]{1,0:T(8,128)S(1)}, u32[]{:S(2)}, u32[]{:S(2)}) %collective-permute-start.4) | collective-permute-done | bytes 131104 | tf_op jit(solution)/shard_map/ppermute | solution.py:377
  58.1 2.9 %collective-permute-start.5 = (f32[32,1024]{1,0:T(8,128)S(1)}, f32[32,1024]{1,0:T(8,128)S(1)}, u32[]{:S(2)}, u32[]{:S(2)}) collective-permute-start(f32[32,1024]{1,0:T(8,128)S(1)} %add.35), channel_id=1, source_target_pairs={{0,16},{4,20},{8,24},{12,28},{16,0},{20,4},{24,8},{28,12},{1,17},{... | collective-permute-start | bytes 393224 | tf_op jit(solution)/shard_map/ppermute | solution.py:377
  61.0 4.5 %collective-permute-done.5 = f32[32,1024]{1,0:T(8,128)S(1)} collective-permute-done((f32[32,1024]{1,0:T(8,128)S(1)}, f32[32,1024]{1,0:T(8,128)S(1)}, u32[]{:S(2)}, u32[]{:S(2)}) %collective-permute-start.5) | collective-permute-done | bytes 131104 | tf_op jit(solution)/shard_map/ppermute | solution.py:377
  70.0 2.1 %collective-permute-done.7.refs_1_ = f32[32,1024]{1,0:T(8,128)} collective-permute-done((f32[32,1024]{1,0:T(8,128)S(1)}, f32[32,1024]{1,0:T(8,128)}, u32[]{:S(2)}, u32[]{:S(2)}) %collective-permute-start.7) | collective-permute-done | bytes 131104 | tf_op jit(solution)/shard_map/ppermute | solution.py:377
  73.8 4.2 %masked_step.1 = (f32[32,1024]{1,0:T(8,128)S(1)}, f32[32,1024]{1,0:T(8,128)S(1)}) custom-call(s32[23]{0:T(128)S(1)} %dynamic-slice_bitcast_fusion.where_ref, s32[2,128]{1,0:T(2,128)S(1)} %bitcast.9, f32[1024,128]{1,0:T(8,128)S(1)} %copy-done.10, f32[32,1024]{1,0:T(8,128)S(1)} %add.36.refs_0_, f32[32,1024]{1,0:T(8,128)} %collective-permute-done.7.refs_1_, ...), custom_call_target="tpu_custom_call" | custom-call | tf_op jit(solution)/shard_map/masked_step/pallas_call | solution.py:160
  78.0 2.1 %collective-permute-start.11 = (f32[32,1024]{1,0:T(8,128)S(1)}, f32[32,1024]{1,0:T(8,128)S(1)}, u32[]{:S(2)}, u32[]{:S(2)}) collective-permute-start(f32[32,1024]{1,0:T(8,128)S(1)} %get-tuple-element.51), channel_id=1, source_target_pairs={{0,4},{4,0},{8,12},{12,8},{16,20},{20,16},{24,28},{28,24},{1,5},{5... | collective-permute-start | bytes 393224 | tf_op jit(solution)/shard_map/ppermute | solution.py:377
  80.1 8.4 %collective-permute-done.11 = f32[32,1024]{1,0:T(8,128)S(1)} collective-permute-done((f32[32,1024]{1,0:T(8,128)S(1)}, f32[32,1024]{1,0:T(8,128)S(1)}, u32[]{:S(2)}, u32[]{:S(2)}) %collective-permute-start.11) | collective-permute-done | bytes 131104 | tf_op jit(solution)/shard_map/ppermute | solution.py:377
  88.7 2.0 %collective-permute-start.32 = (bf16[128,1024]{1,0:T(8,128)(2,1)}, bf16[128,1024]{1,0:T(8,128)(2,1)S(1)}, u32[]{:S(2)}, u32[]{:S(2)}) collective-permute-start(bf16[128,1024]{1,0:T(8,128)(2,1)} %copy-done.5), channel_id=1, source_target_pairs={{0,8},{8,16},{16,24},{24,28},{28,20},{20,12},{12,4},{4,0},{1,9},{9... | collective-permute-start | bytes 786440 | tf_op jit(solution)/shard_map/ppermute | solution.py:360
  90.7 4.3 %collective-permute-done.12 = f32[32,1024]{1,0:T(8,128)S(1)} collective-permute-done((f32[32,1024]{1,0:T(8,128)S(1)}, f32[32,1024]{1,0:T(8,128)S(1)}, u32[]{:S(2)}, u32[]{:S(2)}) %collective-permute-start.12) | collective-permute-done | bytes 131104 | tf_op jit(solution)/shard_map/ppermute | solution.py:377
  95.0 6.9 %collective-permute-done.17.refs_1_ = bf16[128,1024]{1,0:T(8,128)(2,1)S(1)} collective-permute-done((bf16[128,1024]{1,0:T(8,128)(2,1)S(1)}, bf16[128,1024]{1,0:T(8,128)(2,1)S(1)}, u32[]{:S(2)}, u32[]{:S(2)}) %collective-permute-start.17) | collective-permute-done | bytes 262176 | tf_op jit(solution)/shard_map/ppermute | solution.py:360
  102.1 3.5 %collective-permute-start.18 = (bf16[128,1024]{1,0:T(8,128)(2,1)S(1)}, bf16[128,1024]{1,0:T(8,128)(2,1)S(1)}, u32[]{:S(2)}, u32[]{:S(2)}) collective-permute-start(bf16[128,1024]{1,0:T(8,128)(2,1)S(1)} %collective-permute-done.17.refs_1_), channel_id=1, source_target_pairs={{8,0},{16,8},{24,16},{28,24},{20,28},{12,20},{4,12},{0,4},{9,1},{1... | collective-permute-start | bytes 786440 | tf_op jit(solution)/shard_map/ppermute | solution.py:360
  105.6 2.6 %collective-permute-done.21.refs_2_ = bf16[128,1024]{1,0:T(8,128)(2,1)S(1)} collective-permute-done((bf16[128,1024]{1,0:T(8,128)(2,1)}, bf16[128,1024]{1,0:T(8,128)(2,1)S(1)}, u32[]{:S(2)}, u32[]{:S(2)}) %collective-permute-start.21) | collective-permute-done | bytes 262176 | tf_op jit(solution)/shard_map/ppermute | solution.py:360
  108.2 2.4 %collective-permute-done.13 = f32[32,1024]{1,0:T(8,128)S(1)} collective-permute-done((f32[32,1024]{1,0:T(8,128)S(1)}, f32[32,1024]{1,0:T(8,128)S(1)}, u32[]{:S(2)}, u32[]{:S(2)}) %collective-permute-start.13) | collective-permute-done | bytes 131104 | tf_op jit(solution)/shard_map/ppermute | solution.py:377
  113.3 4.4 %shard_map.68.refs_7_ = f32[8,1,512,2048]{3,2,1,0:T(8,128)} custom-call(s32[23]{0:T(128)S(1)} %dynamic-slice_bitcast_fusion.where_ref, bf16[256,1024]{1,0:T(8,128)(2,1)S(1)} %copy-done.1, bf16[128,1024]{1,0:T(8,128)(2,1)S(1)} %get-tuple-element.55.refs_1_.refs_3_, bf16[128,1024]{1,0:T(8,128)(2,1)S(1)} %copy-done.6, ...), custom_call_target="tpu_custom_call" | custom-call | flops 2147483648 | bytes 4194304 | tf_op jit(solution)/shard_map/pallas_call | solution.py:257
  117.8 4.2 %collective-permute-done.14 = f32[32,1024]{1,0:T(8,128)S(1)} collective-permute-done((f32[32,1024]{1,0:T(8,128)S(1)}, f32[32,1024]{1,0:T(8,128)S(1)}, u32[]{:S(2)}, u32[]{:S(2)}) %collective-permute-start.14) | collective-permute-done | bytes 131104 | tf_op jit(solution)/shard_map/ppermute | solution.py:377
  122.0 2.1 %collective-permute-start.22 = (bf16[128,1024]{1,0:T(8,128)(2,1)S(1)}, bf16[128,1024]{1,0:T(8,128)(2,1)S(1)}, u32[]{:S(2)}, u32[]{:S(2)}) collective-permute-start(bf16[128,1024]{1,0:T(8,128)(2,1)S(1)} %collective-permute-done.21.refs_2_), channel_id=1, source_target_pairs={{8,0},{16,8},{24,16},{28,24},{20,28},{12,20},{4,12},{0,4},{9,1},{1... | collective-permute-start | bytes 786440 | tf_op jit(solution)/shard_map/ppermute | solution.py:360
  124.1 4.6 %shard_map.69.refs_7_ = f32[8,1,512,2048]{3,2,1,0:T(8,128)} custom-call(s32[23]{0:T(128)S(1)} %dynamic-slice_bitcast_fusion.where_ref, bf16[256,1024]{1,0:T(8,128)(2,1)} %collective-permute-done.refs_0_, bf16[128,1024]{1,0:T(8,128)(2,1)S(1)} %collective-permute-done.29.refs_1_, ...), custom_call_target="tpu_custom_call", output_to_operand_aliasing={{}: (8, {})} | custom-call | flops 2147483648 | bytes 4194304 | tf_op jit(solution)/shard_map/pallas_call | solution.py:257
  128.7 2.6 %collective-permute-start.24 = (f32[64,1024]{1,0:T(8,128)S(1)}, f32[64,1024]{1,0:T(8,128)S(1)}, u32[]{:S(2)}, u32[]{:S(2)}) collective-permute-start(f32[64,1024]{1,0:T(8,128)S(1)} %pad_maximum_fusion.1), channel_id=1, source_target_pairs={{0,2},{1,3},{2,0},{3,1},{4,6},{5,7},{6,4},{7,5},{8,10},{9,11},{10,... | collective-permute-start | bytes 786440 | tf_op jit(solution)/shard_map/ppermute | solution.py:377
  131.3 4.6 %shard_map.70.refs_7_ = f32[8,1,512,2048]{3,2,1,0:T(8,128)} custom-call(s32[23]{0:T(128)S(1)} %dynamic-slice_bitcast_fusion.where_ref, bf16[256,1024]{1,0:T(8,128)(2,1)} %collective-permute-done.26.refs_0_, bf16[128,1024]{1,0:T(8,128)(2,1)S(1)} %collective-permute-done.17.refs_1_, ...), custom_call_target="tpu_custom_call", output_to_operand_aliasing={{}: (8, {})} | custom-call | flops 2147483648 | bytes 4194304 | tf_op jit(solution)/shard_map/pallas_call | solution.py:257
  135.9 3.6 %collective-permute-start.19 = (bf16[128,1024]{1,0:T(8,128)(2,1)S(1)}, bf16[128,1024]{1,0:T(8,128)(2,1)S(1)}, u32[]{:S(2)}, u32[]{:S(2)}) collective-permute-start(bf16[128,1024]{1,0:T(8,128)(2,1)S(1)} %collective-permute-done.18.refs_1_), channel_id=1, source_target_pairs={{8,0},{16,8},{24,16},{28,24},{20,28},{12,20},{4,12},{0,4},{9,1},{1... | collective-permute-start | bytes 786440 | tf_op jit(solution)/shard_map/ppermute | solution.py:360
  139.5 2.0 %collective-permute-start.23 = (bf16[128,1024]{1,0:T(8,128)(2,1)S(1)}, bf16[128,1024]{1,0:T(8,128)(2,1)S(1)}, u32[]{:S(2)}, u32[]{:S(2)}) collective-permute-start(bf16[128,1024]{1,0:T(8,128)(2,1)S(1)} %collective-permute-done.22.refs_2_), channel_id=1, source_target_pairs={{8,0},{16,8},{24,16},{28,24},{20,28},{12,20},{4,12},{0,4},{9,1},{1... | collective-permute-start | bytes 786440 | tf_op jit(solution)/shard_map/ppermute | solution.py:360
  141.5 4.5 %shard_map.71.refs_7_ = f32[8,1,512,2048]{3,2,1,0:T(8,128)} custom-call(s32[23]{0:T(128)S(1)} %dynamic-slice_bitcast_fusion.where_ref, bf16[256,1024]{1,0:T(8,128)(2,1)S(1)} %collective-permute-done.6.refs_0_, bf16[128,1024]{1,0:T(8,128)(2,1)S(1)} %collective-permute-done.30.refs_1_, ...), custom_call_target="tpu_custom_call", output_to_operand_aliasing={{}: (8, {})} | custom-call | flops 2147483648 | bytes 4194304 | tf_op jit(solution)/shard_map/pallas_call | solution.py:257
  148.4 4.4 %shard_map.72.refs_7_ = f32[8,1,512,2048]{3,2,1,0:T(8,128)} custom-call(s32[23]{0:T(128)S(1)} %dynamic-slice_bitcast_fusion.where_ref, bf16[256,1024]{1,0:T(8,128)(2,1)S(1)} %collective-permute-done.27.refs_0_, bf16[128,1024]{1,0:T(8,128)(2,1)S(1)} %collective-permute-done.18.refs_1_, ...), custom_call_target="tpu_custom_call", output_to_operand_aliasing={{}: (8, {})} | custom-call | flops 2147483648 | bytes 4194304 | tf_op jit(solution)/shard_map/pallas_call | solution.py:257
  154.9 4.0 %collective-permute-done.34.refs_2_ = bf16[128,1024]{1,0:T(8,128)(2,1)S(1)} collective-permute-done((bf16[128,1024]{1,0:T(8,128)(2,1)S(1)}, bf16[128,1024]{1,0:T(8,128)(2,1)S(1)}, u32[]{:S(2)}, u32[]{:S(2)}) %collective-permute-start.34) | collective-permute-done | bytes 262176 | tf_op jit(solution)/shard_map/ppermute | solution.py:360
  158.9 4.4 %shard_map.73.refs_7_ = f32[8,1,512,2048]{3,2,1,0:T(8,128)} custom-call(s32[23]{0:T(128)S(1)} %dynamic-slice_bitcast_fusion.where_ref, bf16[256,1024]{1,0:T(8,128)(2,1)S(1)} %collective-permute-done.15.refs_0_, bf16[128,1024]{1,0:T(8,128)(2,1)S(1)} %collective-permute-done.31.refs_1_, ...), custom_call_target="tpu_custom_call", output_to_operand_aliasing={{}: (8, {})} | custom-call | flops 2147483648 | bytes 4194304 | tf_op jit(solution)/shard_map/pallas_call | solution.py:257
  163.4 4.6 %shard_map.74.refs_7_ = f32[8,1,512,2048]{3,2,1,0:T(8,128)} custom-call(s32[23]{0:T(128)S(1)} %dynamic-slice_bitcast_fusion.where_ref, bf16[256,1024]{1,0:T(8,128)(2,1)S(1)} %collective-permute-done.28.refs_0_, bf16[128,1024]{1,0:T(8,128)(2,1)S(1)} %collective-permute-done.19.refs_1_, ...), custom_call_target="tpu_custom_call", output_to_operand_aliasing={{}: (8, {})} | custom-call | flops 2147483648 | bytes 4194304 | tf_op jit(solution)/shard_map/pallas_call | solution.py:257
  168.0 2.7 %finish.1 = f32[512,256]{1,0:T(8,128)} custom-call(s32[23]{0:T(128)S(1)} %dynamic-slice_bitcast_fusion.where_ref, s32[2,128]{1,0:T(2,128)S(1)} %bitcast.10, f32[512,256]{1,0:T(8,128)S(1)} %copy-done.4, f32[128,1024]{1,0:T(8,128)S(1)} %pad_maximum_fusion.refs_0_, f32[128,1024]{1,0:T(8,128)S(1)} %collective-permute-done.35.refs_1_, ...), custom_call_target="tpu_custom_call" | custom-call | tf_op jit(solution)/shard_map/finish/pallas_call | solution.py:203
  170.7 4.4 %shard_map.75 = f32[8,1,512,2048]{3,2,1,0:T(8,128)} custom-call(s32[23]{0:T(128)S(1)} %dynamic-slice_bitcast_fusion.where_ref, bf16[256,1024]{1,0:T(8,128)(2,1)S(1)} %collective-permute-done.16.refs_0_, bf16[128,1024]{1,0:T(8,128)(2,1)S(1)} %collective-permute-done.20.refs_1_, ...), custom_call_target="tpu_custom_call", output_to_operand_aliasing={{}: (8, {})} | custom-call | flops 2147483648 | bytes 4194304 | tf_op jit(solution)/shard_map/pallas_call | solution.py:257
  (98 shorter events, 29.6 us)
Async XLA Ops:
  14.9 32.1 %collective-permute-start.9 = (bf16[1024,512]{1,0:T(8,128)(2,1)S(1)}, bf16[1024,512]{1,0:T(8,128)(2,1)S(1)}, u32[]{:S(2)}, u32[]{:S(2)}) collective-permute-start(bf16[1024,512]{1,0:T(8,128)(2,1)S(1)} %get-tuple-element.48.refs_2_.refs_3_), channel_id=1, source_target_pairs={{0,2},{1,3},{2,0},{3,1},{4,6},{5,7},{6,4},{7,5},{8,10},{9,11},{10,... | collective-permute-start | bytes 3145736 | tf_op jit(solution)/shard_map/ppermute | solution.py:372
  17.8 29.1 %collective-permute-start.2 = (f32[64,1024]{1,0:T(8,128)S(1)}, f32[64,1024]{1,0:T(8,128)S(1)}, u32[]{:S(2)}, u32[]{:S(2)}) collective-permute-start(f32[64,1024]{1,0:T(8,128)S(1)} %get-tuple-element.41), channel_id=1, source_target_pairs={{0,2},{1,3},{2,0},{3,1},{4,6},{5,7},{6,4},{7,5},{8,10},{9,11},{10,... | collective-permute-start | bytes 786440 | tf_op jit(solution)/shard_map/ppermute | solution.py:377
  46.9 25.2 %collective-permute-start.8 = (bf16[1024,512]{1,0:T(8,128)(2,1)S(1)}, bf16[1024,512]{1,0:T(8,128)(2,1)S(1)}, u32[]{:S(2)}, u32[]{:S(2)}) collective-permute-start(bf16[1024,512]{1,0:T(8,128)(2,1)S(1)} %get-tuple-element.48.refs_2_.refs_3_), channel_id=1, source_target_pairs={{0,1},{1,0},{2,3},{3,2},{4,5},{5,4},{6,7},{7,6},{8,9},{9,8},{10,11... | collective-permute-start | bytes 3145736 | tf_op jit(solution)/shard_map/ppermute | solution.py:372
  47.0 25.1 %collective-permute-start.10 = (bf16[1024,512]{1,0:T(8,128)(2,1)S(1)}, bf16[1024,512]{1,0:T(8,128)(2,1)}, u32[]{:S(2)}, u32[]{:S(2)}) collective-permute-start(bf16[1024,512]{1,0:T(8,128)(2,1)S(1)} %collective-permute-done.9.refs_4_.refs_5_), channel_id=1, source_target_pairs={{0,1},{1,0},{2,3},{3,2},{4,5},{5,4},{6,7},{7,6},{8,9},{9,8},{10,11... | collective-permute-start | bytes 3145736 | tf_op jit(solution)/shard_map/ppermute | solution.py:372
  58.1 7.4 %collective-permute-start.5 = (f32[32,1024]{1,0:T(8,128)S(1)}, f32[32,1024]{1,0:T(8,128)S(1)}, u32[]{:S(2)}, u32[]{:S(2)}) collective-permute-start(f32[32,1024]{1,0:T(8,128)S(1)} %add.35), channel_id=1, source_target_pairs={{0,16},{4,20},{8,24},{12,28},{16,0},{20,4},{24,8},{28,12},{1,17},{... | collective-permute-start | bytes 393224 | tf_op jit(solution)/shard_map/ppermute | solution.py:377
  65.5 6.5 %collective-permute-start.7 = (f32[32,1024]{1,0:T(8,128)S(1)}, f32[32,1024]{1,0:T(8,128)}, u32[]{:S(2)}, u32[]{:S(2)}) collective-permute-start(f32[32,1024]{1,0:T(8,128)S(1)} %add.36.refs_0_), channel_id=1, source_target_pairs={{0,4},{4,0},{8,12},{12,8},{16,20},{20,16},{24,28},{28,24},{1,5},{5... | collective-permute-start | bytes 393224 | tf_op jit(solution)/shard_map/ppermute | solution.py:377
  67.3 34.8 %collective-permute-start = (bf16[256,1024]{1,0:T(8,128)(2,1)}, bf16[256,1024]{1,0:T(8,128)(2,1)}, u32[]{:S(2)}, u32[]{:S(2)}) collective-permute-start(bf16[256,1024]{1,0:T(8,128)(2,1)} %copy-done), channel_id=1, source_target_pairs={{0,8},{8,16},{16,24},{24,28},{28,20},{20,12},{12,4},{4,0},{1,9},{9... | collective-permute-start | bytes 1572872 | tf_op jit(solution)/shard_map/ppermute | solution.py:360
  68.3 33.7 %collective-permute-start.26 = (bf16[256,1024]{1,0:T(8,128)(2,1)}, bf16[256,1024]{1,0:T(8,128)(2,1)}, u32[]{:S(2)}, u32[]{:S(2)}) collective-permute-start(bf16[256,1024]{1,0:T(8,128)(2,1)} %copy-done), channel_id=1, source_target_pairs={{8,0},{16,8},{24,16},{28,24},{20,28},{12,20},{4,12},{0,4},{9,1},{1... | collective-permute-start | bytes 1572872 | tf_op jit(solution)/shard_map/ppermute | solution.py:360
  72.1 16.6 %collective-permute-start.29 = (bf16[128,1024]{1,0:T(8,128)(2,1)S(1)}, bf16[128,1024]{1,0:T(8,128)(2,1)S(1)}, u32[]{:S(2)}, u32[]{:S(2)}) collective-permute-start(bf16[128,1024]{1,0:T(8,128)(2,1)S(1)} %get-tuple-element.55.refs_1_.refs_3_), channel_id=1, source_target_pairs={{0,8},{8,16},{16,24},{24,28},{28,20},{20,12},{12,4},{4,0},{1,9},{9... | collective-permute-start | bytes 786440 | tf_op jit(solution)/shard_map/ppermute | solution.py:360
  78.0 10.5 %collective-permute-start.11 = (f32[32,1024]{1,0:T(8,128)S(1)}, f32[32,1024]{1,0:T(8,128)S(1)}, u32[]{:S(2)}, u32[]{:S(2)}) collective-permute-start(f32[32,1024]{1,0:T(8,128)S(1)} %get-tuple-element.51), channel_id=1, source_target_pairs={{0,4},{4,0},{8,12},{12,8},{16,20},{20,16},{24,28},{28,24},{1,5},{5... | collective-permute-start | bytes 393224 | tf_op jit(solution)/shard_map/ppermute | solution.py:377
  88.6 13.4 %collective-permute-start.17 = (bf16[128,1024]{1,0:T(8,128)(2,1)S(1)}, bf16[128,1024]{1,0:T(8,128)(2,1)S(1)}, u32[]{:S(2)}, u32[]{:S(2)}) collective-permute-start(bf16[128,1024]{1,0:T(8,128)(2,1)S(1)} %get-tuple-element.55.refs_1_.refs_3_), channel_id=1, source_target_pairs={{8,0},{16,8},{24,16},{28,24},{20,28},{12,20},{4,12},{0,4},{9,1},{1... | collective-permute-start | bytes 786440 | tf_op jit(solution)/shard_map/ppermute | solution.py:360
  88.7 16.9 %collective-permute-start.32 = (bf16[128,1024]{1,0:T(8,128)(2,1)}, bf16[128,1024]{1,0:T(8,128)(2,1)S(1)}, u32[]{:S(2)}, u32[]{:S(2)}) collective-permute-start(bf16[128,1024]{1,0:T(8,128)(2,1)} %copy-done.5), channel_id=1, source_target_pairs={{0,8},{8,16},{16,24},{24,28},{28,20},{20,12},{12,4},{4,0},{1,9},{9... | collective-permute-start | bytes 786440 | tf_op jit(solution)/shard_map/ppermute | solution.py:360
  95.0 13.2 %collective-permute-start.21 = (bf16[128,1024]{1,0:T(8,128)(2,1)}, bf16[128,1024]{1,0:T(8,128)(2,1)S(1)}, u32[]{:S(2)}, u32[]{:S(2)}) collective-permute-start(bf16[128,1024]{1,0:T(8,128)(2,1)} %copy-done.5), channel_id=1, source_target_pairs={{8,0},{16,8},{24,16},{28,24},{20,28},{12,20},{4,12},{0,4},{9,1},{1... | collective-permute-start | bytes 786440 | tf_op jit(solution)/shard_map/ppermute | solution.py:360
  102.0 8.7 %collective-permute-start.13 = (f32[32,1024]{1,0:T(8,128)S(1)}, f32[32,1024]{1,0:T(8,128)S(1)}, u32[]{:S(2)}, u32[]{:S(2)}) collective-permute-start(f32[32,1024]{1,0:T(8,128)S(1)} %add.38), channel_id=1, source_target_pairs={{0,16},{4,20},{8,24},{12,28},{16,0},{20,4},{24,8},{28,12},{1,17},{... | collective-permute-start | bytes 393224 | tf_op jit(solution)/shard_map/ppermute | solution.py:377
  102.1 22.0 %collective-permute-start.30 = (bf16[128,1024]{1,0:T(8,128)(2,1)S(1)}, bf16[128,1024]{1,0:T(8,128)(2,1)S(1)}, u32[]{:S(2)}, u32[]{:S(2)}) collective-permute-start(bf16[128,1024]{1,0:T(8,128)(2,1)S(1)} %collective-permute-done.29.refs_1_), channel_id=1, source_target_pairs={{0,8},{8,16},{16,24},{24,28},{28,20},{20,12},{12,4},{4,0},{1,9},{9... | collective-permute-start | bytes 786440 | tf_op jit(solution)/shard_map/ppermute | solution.py:360
  102.1 26.6 %collective-permute-start.18 = (bf16[128,1024]{1,0:T(8,128)(2,1)S(1)}, bf16[128,1024]{1,0:T(8,128)(2,1)S(1)}, u32[]{:S(2)}, u32[]{:S(2)}) collective-permute-start(bf16[128,1024]{1,0:T(8,128)(2,1)S(1)} %collective-permute-done.17.refs_1_), channel_id=1, source_target_pairs={{8,0},{16,8},{24,16},{28,24},{20,28},{12,20},{4,12},{0,4},{9,1},{1... | collective-permute-start | bytes 786440 | tf_op jit(solution)/shard_map/ppermute | solution.py:360
  105.6 16.4 %collective-permute-start.6 = (bf16[256,1024]{1,0:T(8,128)(2,1)}, bf16[256,1024]{1,0:T(8,128)(2,1)S(1)}, u32[]{:S(2)}, u32[]{:S(2)}) collective-permute-start(bf16[256,1024]{1,0:T(8,128)(2,1)} %collective-permute-done.refs_0_), channel_id=1, source_target_pairs={{0,8},{8,16},{16,24},{24,28},{28,20},{20,12},{12,4},{4,0},{1,9},{9... | collective-permute-start | bytes 1572872 | tf_op jit(solution)/shard_map/ppermute | solution.py:360
  108.2 37.8 %collective-permute-start.27 = (bf16[256,1024]{1,0:T(8,128)(2,1)}, bf16[256,1024]{1,0:T(8,128)(2,1)S(1)}, u32[]{:S(2)}, u32[]{:S(2)}) collective-permute-start(bf16[256,1024]{1,0:T(8,128)(2,1)} %collective-permute-done.26.refs_0_), channel_id=1, source_target_pairs={{8,0},{16,8},{24,16},{28,24},{20,28},{12,20},{4,12},{0,4},{9,1},{1... | collective-permute-start | bytes 1572872 | tf_op jit(solution)/shard_map/ppermute | solution.py:360
  110.7 11.3 %collective-permute-start.14 = (f32[32,1024]{1,0:T(8,128)S(1)}, f32[32,1024]{1,0:T(8,128)S(1)}, u32[]{:S(2)}, u32[]{:S(2)}) collective-permute-start(f32[32,1024]{1,0:T(8,128)S(1)} %subtract_add_fusion), channel_id=1, source_target_pairs={{0,4},{4,0},{8,12},{12,8},{16,20},{20,16},{24,28},{28,24},{1,5},{5... | collective-permute-start | bytes 393224 | tf_op jit(solution)/shard_map/ppermute | solution.py:377
  122.0 17.5 %collective-permute-start.33 = (bf16[128,1024]{1,0:T(8,128)(2,1)S(1)}, bf16[128,1024]{1,0:T(8,128)(2,1)S(1)}, u32[]{:S(2)}, u32[]{:S(2)}) collective-permute-start(bf16[128,1024]{1,0:T(8,128)(2,1)S(1)} %collective-permute-done.32.refs_2_), channel_id=1, source_target_pairs={{0,8},{8,16},{16,24},{24,28},{28,20},{20,12},{12,4},{4,0},{1,9},{9... | collective-permute-start | bytes 786440 | tf_op jit(solution)/shard_map/ppermute | solution.py:360
  122.0 13.9 %collective-permute-start.22 = (bf16[128,1024]{1,0:T(8,128)(2,1)S(1)}, bf16[128,1024]{1,0:T(8,128)(2,1)S(1)}, u32[]{:S(2)}, u32[]{:S(2)}) collective-permute-start(bf16[128,1024]{1,0:T(8,128)(2,1)S(1)} %collective-permute-done.21.refs_2_), channel_id=1, source_target_pairs={{8,0},{16,8},{24,16},{28,24},{20,28},{12,20},{4,12},{0,4},{9,1},{1... | collective-permute-start | bytes 786440 | tf_op jit(solution)/shard_map/ppermute | solution.py:360
  124.1 22.1 %collective-permute-start.15 = (bf16[256,1024]{1,0:T(8,128)(2,1)S(1)}, bf16[256,1024]{1,0:T(8,128)(2,1)S(1)}, u32[]{:S(2)}, u32[]{:S(2)}) collective-permute-start(bf16[256,1024]{1,0:T(8,128)(2,1)S(1)} %collective-permute-done.6.refs_0_), channel_id=1, source_target_pairs={{0,8},{8,16},{16,24},{24,28},{28,20},{20,12},{12,4},{4,0},{1,9},{9... | collective-permute-start | bytes 1572872 | tf_op jit(solution)/shard_map/ppermute | solution.py:360
  128.7 17.4 %collective-permute-start.24 = (f32[64,1024]{1,0:T(8,128)S(1)}, f32[64,1024]{1,0:T(8,128)S(1)}, u32[]{:S(2)}, u32[]{:S(2)}) collective-permute-start(f32[64,1024]{1,0:T(8,128)S(1)} %pad_maximum_fusion.1), channel_id=1, source_target_pairs={{0,2},{1,3},{2,0},{3,1},{4,6},{5,7},{6,4},{7,5},{8,10},{9,11},{10,... | collective-permute-start | bytes 786440 | tf_op jit(solution)/shard_map/ppermute | solution.py:377
  135.9 12.3 %collective-permute-start.19 = (bf16[128,1024]{1,0:T(8,128)(2,1)S(1)}, bf16[128,1024]{1,0:T(8,128)(2,1)S(1)}, u32[]{:S(2)}, u32[]{:S(2)}) collective-permute-start(bf16[128,1024]{1,0:T(8,128)(2,1)S(1)} %collective-permute-done.18.refs_1_), channel_id=1, source_target_pairs={{8,0},{16,8},{24,16},{28,24},{20,28},{12,20},{4,12},{0,4},{9,1},{1... | collective-permute-start | bytes 786440 | tf_op jit(solution)/shard_map/ppermute | solution.py:360
  139.5 8.8 %collective-permute-start.23 = (bf16[128,1024]{1,0:T(8,128)(2,1)S(1)}, bf16[128,1024]{1,0:T(8,128)(2,1)S(1)}, u32[]{:S(2)}, u32[]{:S(2)}) collective-permute-start(bf16[128,1024]{1,0:T(8,128)(2,1)S(1)} %collective-permute-done.22.refs_2_), channel_id=1, source_target_pairs={{8,0},{16,8},{24,16},{28,24},{20,28},{12,20},{4,12},{0,4},{9,1},{1... | collective-permute-start | bytes 786440 | tf_op jit(solution)/shard_map/ppermute | solution.py:360
  146.0 7.3 %collective-permute-start.31 = (bf16[128,1024]{1,0:T(8,128)(2,1)S(1)}, bf16[128,1024]{1,0:T(8,128)(2,1)S(1)}, u32[]{:S(2)}, u32[]{:S(2)}) collective-permute-start(bf16[128,1024]{1,0:T(8,128)(2,1)S(1)} %collective-permute-done.30.refs_1_), channel_id=1, source_target_pairs={{0,8},{8,16},{16,24},{24,28},{28,20},{20,12},{12,4},{4,0},{1,9},{9... | collective-permute-start | bytes 786440 | tf_op jit(solution)/shard_map/ppermute | solution.py:360
  146.1 12.8 %collective-permute-start.34 = (bf16[128,1024]{1,0:T(8,128)(2,1)S(1)}, bf16[128,1024]{1,0:T(8,128)(2,1)S(1)}, u32[]{:S(2)}, u32[]{:S(2)}) collective-permute-start(bf16[128,1024]{1,0:T(8,128)(2,1)S(1)} %collective-permute-done.33.refs_2_), channel_id=1, source_target_pairs={{0,8},{8,16},{16,24},{24,28},{28,20},{20,12},{12,4},{4,0},{1,9},{9... | collective-permute-start | bytes 786440 | tf_op jit(solution)/shard_map/ppermute | solution.py:360
  146.2 17.2 %collective-permute-start.28 = (bf16[256,1024]{1,0:T(8,128)(2,1)S(1)}, bf16[256,1024]{1,0:T(8,128)(2,1)S(1)}, u32[]{:S(2)}, u32[]{:S(2)}) collective-permute-start(bf16[256,1024]{1,0:T(8,128)(2,1)S(1)} %collective-permute-done.27.refs_0_), channel_id=1, source_target_pairs={{8,0},{16,8},{24,16},{28,24},{20,28},{12,20},{4,12},{0,4},{9,1},{1... | collective-permute-start | bytes 1572872 | tf_op jit(solution)/shard_map/ppermute | solution.py:360
  148.2 19.7 %collective-permute-start.35 = (f32[128,1024]{1,0:T(8,128)S(1)}, f32[128,1024]{1,0:T(8,128)S(1)}, u32[]{:S(2)}, u32[]{:S(2)}) collective-permute-start(f32[128,1024]{1,0:T(8,128)S(1)} %pad_maximum_fusion.refs_0_), channel_id=1, source_target_pairs={{0,1},{1,0},{2,3},{3,2},{4,5},{5,4},{6,7},{7,6},{8,9},{9,8},{10,11... | collective-permute-start | bytes 1572872 | tf_op jit(solution)/shard_map/ppermute | solution.py:377
  148.3 22.4 %collective-permute-start.16 = (bf16[256,1024]{1,0:T(8,128)(2,1)S(1)}, bf16[256,1024]{1,0:T(8,128)(2,1)S(1)}, u32[]{:S(2)}, u32[]{:S(2)}) collective-permute-start(bf16[256,1024]{1,0:T(8,128)(2,1)S(1)} %collective-permute-done.15.refs_0_), channel_id=1, source_target_pairs={{0,8},{8,16},{16,24},{24,28},{28,20},{20,12},{12,4},{4,0},{1,9},{9... | collective-permute-start | bytes 1572872 | tf_op jit(solution)/shard_map/ppermute | solution.py:360
  153.3 17.4 %collective-permute-start.20 = (bf16[128,1024]{1,0:T(8,128)(2,1)S(1)}, bf16[128,1024]{1,0:T(8,128)(2,1)S(1)}, u32[]{:S(2)}, u32[]{:S(2)}) collective-permute-start(bf16[128,1024]{1,0:T(8,128)(2,1)S(1)} %collective-permute-done.19.refs_1_), channel_id=1, source_target_pairs={{8,0},{16,8},{24,16},{28,24},{20,28},{12,20},{4,12},{0,4},{9,1},{1... | collective-permute-start | bytes 786440 | tf_op jit(solution)/shard_map/ppermute | solution.py:360
  158.9 11.8 %collective-permute-start.25 = (bf16[128,1024]{1,0:T(8,128)(2,1)S(1)}, bf16[128,1024]{1,0:T(8,128)(2,1)S(1)}, u32[]{:S(2)}, u32[]{:S(2)}) collective-permute-start(bf16[128,1024]{1,0:T(8,128)(2,1)S(1)} %collective-permute-done.23.refs_2_), channel_id=1, source_target_pairs={{8,0},{16,8},{24,16},{28,24},{20,28},{12,20},{4,12},{0,4},{9,1},{1... | collective-permute-start | bytes 786440 | tf_op jit(solution)/shard_map/ppermute | solution.py:360
  (22 other events, 46.2 us)
